TPU v7x, 32 devices: a whole 2x2x4 slice. The times are simulated.
32 devices in a mesh: inst: 16 (over z, y, x), cells: 2 (over core).
Axes of the slice: x: 2, y: 2, z: 4, core: 2. Of those that a mesh axis runs over, the one named last changes fastest.
Arguments:
- adjoint: float32 [16, 5, 8, 16, 128], P('inst', None, 'cells'), may hold values from -6 to 6
- objective_gradient: float32 [16, 5, 8, 16, 128], P('inst', None, 'cells'), may hold values from -6 to 6
- jacobian: float32 [16, 3, 5, 5, 8, 16, 128], P('inst', None, None, None, 'cells'), may hold values from -2.5 to 2.5
- second_coef: float32 [16, 3, 8, 16, 128], P('inst', None, 'cells'), may hold values from 0.05 to 0.5
- fourth_coef: float32 [16, 3, 8, 16, 128], P('inst', None, 'cells'), may hold values from 0.01 to 0.1
- time_step: float32 [16, 8, 16, 128], P('inst', 'cells'), may hold values from 0.03 to 0.15
- frequency: float32 [1], replicated, may hold values from 0.5 to 1.5
- damping: float32 [1], replicated, may hold values from 0.02 to 0.08
Outputs:
- updated: float32 [16, 5, 8, 16, 128], P('inst', None, 'cells')
All inputs are finite; a program needn't handle non-finite values.
Results may differ from a plain program's by a relative error of at most 0.0001.
Values sent between devices are 32-bit elements; how exact they have to be, the bound alone decides.
A program may use at most 64 MiB of HBM per device.

v0:
```python
import math

import jax
import jax.numpy as jnp
from jax import lax
from jax.sharding import PartitionSpec as P

INSTANCES = 16


def padded_2(array, sides, width):
    for axis, dim in sides:
        devices, length = (lax.axis_size(axis), array.shape[dim])
        up = [(i, (i + 1) % devices) for i in range(devices - 1)]
        down = [(j, i) for i, j in up]
        last = lax.slice_in_dim(array, length - width, length, axis=dim)
        initial = lax.slice_in_dim(array, 0, width, axis=dim)
        before = lax.ppermute(last, axis, up)
        after = lax.ppermute(initial, axis, down)
        array = jnp.concatenate([before, array, after], axis=dim)
    return array


def spectral_coupling(frequency_value, damping_value, count):
    positions = jnp.arange(count, dtype=jnp.int32)
    offsets = positions[:, None] - positions[None, :]
    parity = jnp.where(offsets % 2 == 0, 1.0, -1.0).astype(jnp.float32)
    angle = math.pi / count * offsets.astype(jnp.float32)
    off_diag = offsets != 0
    sine = jnp.where(off_diag, jnp.sin(angle), 1.0)
    slope = jnp.where(off_diag, 0.5 * parity * jnp.cos(angle) / sine, 0.0)
    curve = jnp.where(off_diag, parity * 0.5 / (sine * sine), count * count / 12.0 + 1.0 / 6.0)
    return frequency_value * slope + damping_value * curve


def face_terms(padded, second_pad, fourth_pad, grid_axis):
    length = padded.shape[grid_axis] - 4

    def cut(source, first, size):
        return lax.slice_in_dim(source, first, first + size, axis=grid_axis)

    jumps = cut(padded, 1, length + 3) - cut(padded, 0, length + 3)
    second_flux = cut(second_pad, 0, length + 3) * jumps
    fourth_flux = cut(fourth_pad, 0, length + 3) * jumps
    divided = cut(fourth_flux, 1, length + 2) - cut(fourth_flux, 0, length + 2)
    central = 0.5 * (cut(padded, 1, length) - cut(padded, 3, length))
    damped = cut(second_flux, 1, length) - cut(second_flux, 2, length)
    damped = (
        damped + cut(divided, 2, length) - 2.0 * cut(divided, 1, length) + cut(divided, 0, length)
    )
    return (central, damped)


def on_device(
    adjoint, objective_gradient, jacobian, second_coef, fourth_coef, time_step, frequency, damping
):
    coupling = spectral_coupling(frequency[0], damping[0], INSTANCES)
    stacked = jnp.stack([second_coef[:, 0], fourth_coef[:, 0]], axis=1)
    coef_rim = padded_2(stacked, (("cells", 2),), 2)
    second_pads = [coef_rim[:, 0:1]]
    fourth_pads = [coef_rim[:, 1:2]]
    for direction in (1, 2):
        widths = [(0, 0), (0, 0), (0, 0), (0, 0), (0, 0)]
        widths[2 + direction] = (2, 2)
        second_pads.append(jnp.pad(second_coef[:, direction][:, None], widths))
        fourth_pads.append(jnp.pad(fourth_coef[:, direction][:, None], widths))
    section_state = adjoint
    for section_coef in (0.25, 1.0 / 6.0, 0.375, 0.5, 1.0):
        summed = jnp.zeros_like(section_state)
        for spatial_direction in range(3):
            grid_axis = 2 + spatial_direction
            if spatial_direction == 0:
                padded = padded_2(section_state, (("cells", 2),), 2)
            else:
                spatial_widths = [(0, 0), (0, 0), (0, 0), (0, 0), (0, 0)]
                spatial_widths[grid_axis] = (2, 2)
                padded = jnp.pad(section_state, spatial_widths)
            central, damped = face_terms(
                padded, second_pads[spatial_direction], fourth_pads[spatial_direction], grid_axis
            )
            summed = (
                summed
                + jnp.sum(jacobian[:, spatial_direction] * central[:, :, None], axis=1)
                + damped
            )
        mixed = jnp.einsum(
            "jk,jvxyz->kvxyz",
            coupling,
            lax.all_to_all(section_state, "inst", split_axis=3, concat_axis=0, tiled=True),
            precision=lax.Precision.HIGHEST,
        )
        residual = (
            summed
            + lax.all_to_all(mixed, "inst", split_axis=0, concat_axis=3, tiled=True)
            + objective_gradient
        )
        section_state = adjoint - section_coef * time_step[:, None] * residual
    return section_state


def solution(mesh):
    placed = (
        P("inst", None, "cells", None, None),
        P("inst", None, "cells", None, None),
        P("inst", None, None, None, "cells", None, None),
        P("inst", None, "cells", None, None),
        P("inst", None, "cells", None, None),
        P("inst", "cells", None, None),
        P(),
        P(),
    )
    return jax.shard_map(
        on_device,
        mesh=mesh,
        in_specs=placed,
        out_specs=P("inst", None, "cells", None, None),
        check_vma=False,
    )
```

profile of v0, /device:TPU:0, one launch (start us, length us, event | category | flops | bytes accessed | tf_op | source)
XLA Modules:
  0.0 202.0 jit_solution(2425450394038306500)
XLA Ops:
  2.2 2.4 %collective-permute-start.2 = (f32[1,2,2,16,128]{4,3,2,1,0:T(8,128)}, f32[1,2,2,16,128]{4,3,2,1,0:T(8,128)S(1)}, u32[]{:S(2)}, u32[]{:S(2)}) collective-permute-start(f32[1,2,2,16,128]{4,3,2,1,0:T(8,128)} %get-tuple-element.84), channel_id=1, source_target_pairs={{0,1},{2,3},{4,5},{6,7},{8,9},{10,11},{12,13},{14,15},{16,17},{18,... | collective-permute-start | bytes 98312 | tf_op jit(solution)/shard_map/ppermute | solution.py:18
  7.5 3.7 %collective-permute-start = (f32[1,5,2,16,128]{4,3,2,1,0:T(8,128)}, f32[1,5,2,16,128]{4,3,2,1,0:T(8,128)S(1)}, u32[]{:S(2)}, u32[]{:S(2)}) collective-permute-start(f32[1,5,2,16,128]{4,3,2,1,0:T(8,128)} %get-tuple-element.71), channel_id=1, source_target_pairs={{0,1},{2,3},{4,5},{6,7},{8,9},{10,11},{12,13},{14,15},{16,17},{18,... | collective-permute-start | bytes 245768 | tf_op jit(solution)/shard_map/ppermute | solution.py:18
  14.3 7.7 %all-to-all-start = ((f32[1,5,4,16,128]{4,1,2,0,3:T(8,128)}), f32[1,5,4,16,128]{4,1,2,0,3:T(8,128)}, u32[]{:S(2)}, u32[]{:S(2)}) async-start(f32[1,5,4,16,128]{4,1,2,0,3:T(8,128)} %copy.68), calls=%async_computation | async-start | bytes 524288 | tf_op jit(solution)/shard_map/all_to_all | solution.py:89
  34.9 5.5 %all-to-all-start.1 = ((f32[16,5,4,1,128]{4,2,1,3,0:T(4,128)}), f32[16,5,4,1,128]{4,2,1,3,0:T(4,128)}, u32[]{:S(2)}, u32[]{:S(2)}) async-start(f32[16,5,4,1,128]{4,2,1,3,0:T(4,128)} %copy.70), calls=%async_computation.1 | async-start | bytes 327680 | tf_op jit(solution)/shard_map/all_to_all | solution.py:94
  43.3 5.7 %all-to-all-done.1 = f32[16,5,4,1,128]{4,2,1,3,0:T(4,128)} async-done(((f32[16,5,4,1,128]{4,2,1,3,0:T(4,128)}), f32[16,5,4,1,128]{4,2,1,3,0:T(4,128)}, u32[]{:S(2)}, u32[]{:S(2)}) %all-to-all-start.1) | async-done | bytes 163872 | tf_op jit(solution)/shard_map/all_to_all | solution.py:94
  58.8 4.2 %all-to-all-start.2 = ((f32[1,5,4,16,128]{4,2,1,0,3:T(4,128)}), f32[1,5,4,16,128]{4,2,1,0,3:T(4,128)}, u32[]{:S(2)}, u32[]{:S(2)}) async-start(f32[1,5,4,16,128]{4,2,1,0,3:T(4,128)} %copy.72), calls=%async_computation.2 | async-start | bytes 327680 | tf_op jit(solution)/shard_map/all_to_all | solution.py:89
  67.1 4.1 %all-to-all-done.2 = f32[1,5,4,16,128]{4,2,1,0,3:T(4,128)} async-done(((f32[1,5,4,16,128]{4,2,1,0,3:T(4,128)}), f32[1,5,4,16,128]{4,2,1,0,3:T(4,128)}, u32[]{:S(2)}, u32[]{:S(2)}) %all-to-all-start.2) | async-done | bytes 163872 | tf_op jit(solution)/shard_map/all_to_all | solution.py:89
  73.2 4.2 %all-to-all-start.3 = ((f32[16,5,4,1,128]{4,2,1,3,0:T(4,128)}), f32[16,5,4,1,128]{4,2,1,3,0:T(4,128)}, u32[]{:S(2)}, u32[]{:S(2)}) async-start(f32[16,5,4,1,128]{4,2,1,3,0:T(4,128)} %copy.74), calls=%async_computation.3 | async-start | bytes 327680 | tf_op jit(solution)/shard_map/all_to_all | solution.py:94
  80.3 5.9 %all-to-all-done.3 = f32[16,5,4,1,128]{4,2,1,3,0:T(4,128)} async-done(((f32[16,5,4,1,128]{4,2,1,3,0:T(4,128)}), f32[16,5,4,1,128]{4,2,1,3,0:T(4,128)}, u32[]{:S(2)}, u32[]{:S(2)}) %all-to-all-start.3) | async-done | bytes 163872 | tf_op jit(solution)/shard_map/all_to_all | solution.py:94
  86.3 2.3 %fusion.104 = f32[1,5,4,16,128]{4,3,2,1,0:T(8,128)S(1)} fusion(f32[1,5,4,16,128]{4,3,2,1,0:T(8,128)S(1)} %copy-done.1, f32[1,5,4,16,128]{4,3,2,1,0:T(8,128)S(1)} %copy-done.2, f32[1,5,4,16,130]{4,3,2,1,0:T(8,128)} %slice_subtract_fusion.3, f32[1,5,4,16,131]{4,3,2,1,0:T(8,128)} %get-tuple-element.64, f32[1,5,4,18,128]{4,3,2,1,0:T(8,128)S(1)} %slice_subtract_fusion.16, ...), kind=kLoop, calls=%fused_computation.231 | loop fusion | flops 983040 | bytes 3637248 | tf_op jit(solution)/shard_map/sub | solution.py:97
  96.6 4.2 %all-to-all-start.4 = ((f32[1,5,4,16,128]{4,2,1,0,3:T(4,128)}), f32[1,5,4,16,128]{4,2,1,0,3:T(4,128)}, u32[]{:S(2)}, u32[]{:S(2)}) async-start(f32[1,5,4,16,128]{4,2,1,0,3:T(4,128)} %copy.76), calls=%async_computation.4 | async-start | bytes 327680 | tf_op jit(solution)/shard_map/all_to_all | solution.py:89
  104.9 4.1 %all-to-all-done.4 = f32[1,5,4,16,128]{4,2,1,0,3:T(4,128)} async-done(((f32[1,5,4,16,128]{4,2,1,0,3:T(4,128)}), f32[1,5,4,16,128]{4,2,1,0,3:T(4,128)}, u32[]{:S(2)}, u32[]{:S(2)}) %all-to-all-start.4) | async-done | bytes 163872 | tf_op jit(solution)/shard_map/all_to_all | solution.py:89
  111.0 4.2 %all-to-all-start.5 = ((f32[16,5,4,1,128]{4,2,1,3,0:T(4,128)}), f32[16,5,4,1,128]{4,2,1,3,0:T(4,128)}, u32[]{:S(2)}, u32[]{:S(2)}) async-start(f32[16,5,4,1,128]{4,2,1,3,0:T(4,128)} %copy.78), calls=%async_computation.5 | async-start | bytes 327680 | tf_op jit(solution)/shard_map/all_to_all | solution.py:94
  118.1 5.9 %all-to-all-done.5 = f32[16,5,4,1,128]{4,2,1,3,0:T(4,128)} async-done(((f32[16,5,4,1,128]{4,2,1,3,0:T(4,128)}), f32[16,5,4,1,128]{4,2,1,3,0:T(4,128)}, u32[]{:S(2)}, u32[]{:S(2)}) %all-to-all-start.5) | async-done | bytes 163872 | tf_op jit(solution)/shard_map/all_to_all | solution.py:94
  134.4 4.2 %all-to-all-start.6 = ((f32[1,5,4,16,128]{4,2,1,0,3:T(4,128)}), f32[1,5,4,16,128]{4,2,1,0,3:T(4,128)}, u32[]{:S(2)}, u32[]{:S(2)}) async-start(f32[1,5,4,16,128]{4,2,1,0,3:T(4,128)} %copy.80), calls=%async_computation.6 | async-start | bytes 327680 | tf_op jit(solution)/shard_map/all_to_all | solution.py:89
  142.7 4.1 %all-to-all-done.6 = f32[1,5,4,16,128]{4,2,1,0,3:T(4,128)} async-done(((f32[1,5,4,16,128]{4,2,1,0,3:T(4,128)}), f32[1,5,4,16,128]{4,2,1,0,3:T(4,128)}, u32[]{:S(2)}, u32[]{:S(2)}) %all-to-all-start.6) | async-done | bytes 163872 | tf_op jit(solution)/shard_map/all_to_all | solution.py:89
  148.8 4.2 %all-to-all-start.7 = ((f32[16,5,4,1,128]{4,2,1,3,0:T(4,128)}), f32[16,5,4,1,128]{4,2,1,3,0:T(4,128)}, u32[]{:S(2)}, u32[]{:S(2)}) async-start(f32[16,5,4,1,128]{4,2,1,3,0:T(4,128)} %copy.82), calls=%async_computation.7 | async-start | bytes 327680 | tf_op jit(solution)/shard_map/all_to_all | solution.py:94
  155.9 5.9 %all-to-all-done.7 = f32[16,5,4,1,128]{4,2,1,3,0:T(4,128)} async-done(((f32[16,5,4,1,128]{4,2,1,3,0:T(4,128)}), f32[16,5,4,1,128]{4,2,1,3,0:T(4,128)}, u32[]{:S(2)}, u32[]{:S(2)}) %all-to-all-start.7) | async-done | bytes 163872 | tf_op jit(solution)/shard_map/all_to_all | solution.py:94
  161.8 2.3 %fusion.74 = f32[1,5,4,16,128]{4,3,2,1,0:T(8,128)S(1)} fusion(f32[1,5,4,16,128]{4,3,2,1,0:T(8,128)S(1)} %copy-done.1, f32[1,5,4,16,128]{4,3,2,1,0:T(8,128)S(1)} %copy-done.2, f32[1,5,4,16,130]{4,3,2,1,0:T(8,128)} %slice_subtract_fusion.1, f32[1,5,4,16,131]{4,3,2,1,0:T(8,128)} %get-tuple-element.46, f32[1,5,4,18,128]{4,3,2,1,0:T(8,128)S(1)} %slice_subtract_fusion.12, ...), kind=kLoop, calls=%fused_computation.173 | loop fusion | flops 983040 | bytes 3637248 | tf_op jit(solution)/shard_map/sub | solution.py:97
  172.2 4.2 %all-to-all-start.8 = ((f32[1,5,4,16,128]{4,2,1,0,3:T(4,128)}), f32[1,5,4,16,128]{4,2,1,0,3:T(4,128)}, u32[]{:S(2)}, u32[]{:S(2)}) async-start(f32[1,5,4,16,128]{4,2,1,0,3:T(4,128)} %copy.84), calls=%async_computation.8 | async-start | bytes 327680 | tf_op jit(solution)/shard_map/all_to_all | solution.py:89
  179.7 4.9 %all-to-all-done.8 = f32[1,5,4,16,128]{4,2,1,0,3:T(4,128)} async-done(((f32[1,5,4,16,128]{4,2,1,0,3:T(4,128)}), f32[1,5,4,16,128]{4,2,1,0,3:T(4,128)}, u32[]{:S(2)}, u32[]{:S(2)}) %all-to-all-start.8) | async-done | bytes 163872 | tf_op jit(solution)/shard_map/all_to_all | solution.py:89
  186.6 4.1 %all-to-all-start.9 = ((f32[16,5,4,1,128]{4,2,1,3,0:T(4,128)}), f32[16,5,4,1,128]{4,2,1,3,0:T(4,128)S(1)}, u32[]{:S(2)}, u32[]{:S(2)}) async-start(f32[16,5,4,1,128]{4,2,1,3,0:T(4,128)} %copy.86), calls=%async_computation.9 | async-start | bytes 327680 | tf_op jit(solution)/shard_map/all_to_all | solution.py:94
  193.0 6.3 %all-to-all-done.9 = f32[16,5,4,1,128]{4,2,1,3,0:T(4,128)S(1)} async-done(((f32[16,5,4,1,128]{4,2,1,3,0:T(4,128)}), f32[16,5,4,1,128]{4,2,1,3,0:T(4,128)S(1)}, u32[]{:S(2)}, u32[]{:S(2)}) %all-to-all-start.9) | async-done | bytes 163872 | tf_op jit(solution)/shard_map/all_to_all | solution.py:94
  199.2 2.8 %fusion.59 = f32[1,5,4,16,128]{4,3,2,1,0:T(8,128)} fusion(f32[1,5,4,16,128]{4,3,2,1,0:T(8,128)S(1)} %copy-done.1, f32[1,5,4,16,128]{4,3,2,1,0:T(8,128)S(1)} %copy-done.2, f32[1,5,4,16,130]{4,3,2,1,0:T(8,128)} %slice_subtract_fusion, f32[1,5,4,16,131]{4,3,2,1,0:T(8,128)} %get-tuple-element.37, f32[1,5,4,18,128]{4,3,2,1,0:T(8,128)S(1)} %slice_subtract_fusion.10, ...), kind=kLoop, calls=%fused_computation.144 | loop fusion | flops 983040 | bytes 3637248 | tf_op jit(solution)/shard_map/sub | solution.py:97
  (116 shorter events, 93.5 us)
Async XLA Ops:
  0.0 24.3 %copy-start.1 = (f32[1,5,4,16,128]{4,3,2,1,0:T(8,128)S(1)}, f32[1,5,4,16,128]{4,3,2,1,0:T(8,128)}, u32[]{:S(2)}) copy-start(f32[1,5,4,16,128]{4,3,2,1,0:T(8,128)} %param.8) | copy-start | bytes 491524
  2.2 26.0 %collective-permute-start.2 = (f32[1,2,2,16,128]{4,3,2,1,0:T(8,128)}, f32[1,2,2,16,128]{4,3,2,1,0:T(8,128)S(1)}, u32[]{:S(2)}, u32[]{:S(2)}) collective-permute-start(f32[1,2,2,16,128]{4,3,2,1,0:T(8,128)} %get-tuple-element.84), channel_id=1, source_target_pairs={{0,1},{2,3},{4,5},{6,7},{8,9},{10,11},{12,13},{14,15},{16,17},{18,... | collective-permute-start | bytes 98312 | tf_op jit(solution)/shard_map/ppermute | solution.py:18
  4.6 24.2 %collective-permute-start.3 = (f32[1,2,2,16,128]{4,3,2,1,0:T(8,128)S(1)}, f32[1,2,2,16,128]{4,3,2,1,0:T(8,128)}, u32[]{:S(2)}, u32[]{:S(2)}) collective-permute-start(f32[1,2,2,16,128]{4,3,2,1,0:T(8,128)S(1)} %get-tuple-element.85), channel_id=1, source_target_pairs={{1,0},{3,2},{5,4},{7,6},{9,8},{11,10},{13,12},{15,14},{17,16},{19,... | collective-permute-start | bytes 98312 | tf_op jit(solution)/shard_map/ppermute | solution.py:19
  7.5 18.7 %copy-start.6 = (f32[1,4,16,128]{3,2,1,0:T(8,128)S(1)}, f32[1,4,16,128]{3,2,1,0:T(8,128)}, u32[]{:S(2)}) copy-start(f32[1,4,16,128]{3,2,1,0:T(8,128)} %param.13) | copy-start | bytes 98308
  7.5 22.1 %collective-permute-start = (f32[1,5,2,16,128]{4,3,2,1,0:T(8,128)}, f32[1,5,2,16,128]{4,3,2,1,0:T(8,128)S(1)}, u32[]{:S(2)}, u32[]{:S(2)}) collective-permute-start(f32[1,5,2,16,128]{4,3,2,1,0:T(8,128)} %get-tuple-element.71), channel_id=1, source_target_pairs={{0,1},{2,3},{4,5},{6,7},{8,9},{10,11},{12,13},{14,15},{16,17},{18,... | collective-permute-start | bytes 245768 | tf_op jit(solution)/shard_map/ppermute | solution.py:18
  11.3 18.4 %collective-permute-start.1 = (f32[1,5,2,16,128]{4,3,2,1,0:T(8,128)}, f32[1,5,2,16,128]{4,3,2,1,0:T(8,128)S(1)}, u32[]{:S(2)}, u32[]{:S(2)}) collective-permute-start(f32[1,5,2,16,128]{4,3,2,1,0:T(8,128)} %get-tuple-element.70), channel_id=1, source_target_pairs={{1,0},{3,2},{5,4},{7,6},{9,8},{11,10},{13,12},{15,14},{17,16},{19,... | collective-permute-start | bytes 245768 | tf_op jit(solution)/shard_map/ppermute | solution.py:19
  14.3 18.5 %all-to-all-start = ((f32[1,5,4,16,128]{4,1,2,0,3:T(8,128)}), f32[1,5,4,16,128]{4,1,2,0,3:T(8,128)}, u32[]{:S(2)}, u32[]{:S(2)}) async-start(f32[1,5,4,16,128]{4,1,2,0,3:T(8,128)} %copy.68), calls=%async_computation | async-start | bytes 524288 | tf_op jit(solution)/shard_map/all_to_all | solution.py:89
  34.9 14.1 %all-to-all-start.1 = ((f32[16,5,4,1,128]{4,2,1,3,0:T(4,128)}), f32[16,5,4,1,128]{4,2,1,3,0:T(4,128)}, u32[]{:S(2)}, u32[]{:S(2)}) async-start(f32[16,5,4,1,128]{4,2,1,3,0:T(4,128)} %copy.70), calls=%async_computation.1 | async-start | bytes 327680 | tf_op jit(solution)/shard_map/all_to_all | solution.py:94
  54.5 8.4 %collective-permute-start.4 = (f32[1,5,2,16,128]{4,3,2,1,0:T(8,128)}, f32[1,5,2,16,128]{4,3,2,1,0:T(8,128)S(1)}, u32[]{:S(2)}, u32[]{:S(2)}) collective-permute-start(f32[1,5,2,16,128]{4,3,2,1,0:T(8,128)} %get-tuple-element.60), channel_id=1, source_target_pairs={{0,1},{2,3},{4,5},{6,7},{8,9},{10,11},{12,13},{14,15},{16,17},{18,... | collective-permute-start | bytes 245768 | tf_op jit(solution)/shard_map/ppermute | solution.py:18
  55.8 7.1 %collective-permute-start.5 = (f32[1,5,2,16,128]{4,3,2,1,0:T(8,128)}, f32[1,5,2,16,128]{4,3,2,1,0:T(8,128)}, u32[]{:S(2)}, u32[]{:S(2)}) collective-permute-start(f32[1,5,2,16,128]{4,3,2,1,0:T(8,128)} %get-tuple-element.61), channel_id=1, source_target_pairs={{1,0},{3,2},{5,4},{7,6},{9,8},{11,10},{13,12},{15,14},{17,16},{19,... | collective-permute-start | bytes 245768 | tf_op jit(solution)/shard_map/ppermute | solution.py:19
  58.8 12.4 %all-to-all-start.2 = ((f32[1,5,4,16,128]{4,2,1,0,3:T(4,128)}), f32[1,5,4,16,128]{4,2,1,0,3:T(4,128)}, u32[]{:S(2)}, u32[]{:S(2)}) async-start(f32[1,5,4,16,128]{4,2,1,0,3:T(4,128)} %copy.72), calls=%async_computation.2 | async-start | bytes 327680 | tf_op jit(solution)/shard_map/all_to_all | solution.py:89
  73.2 13.1 %all-to-all-start.3 = ((f32[16,5,4,1,128]{4,2,1,3,0:T(4,128)}), f32[16,5,4,1,128]{4,2,1,3,0:T(4,128)}, u32[]{:S(2)}, u32[]{:S(2)}) async-start(f32[16,5,4,1,128]{4,2,1,3,0:T(4,128)} %copy.74), calls=%async_computation.3 | async-start | bytes 327680 | tf_op jit(solution)/shard_map/all_to_all | solution.py:94
  91.9 8.9 %collective-permute-start.6 = (f32[1,5,2,16,128]{4,3,2,1,0:T(8,128)}, f32[1,5,2,16,128]{4,3,2,1,0:T(8,128)S(1)}, u32[]{:S(2)}, u32[]{:S(2)}) collective-permute-start(f32[1,5,2,16,128]{4,3,2,1,0:T(8,128)} %get-tuple-element.51), channel_id=1, source_target_pairs={{0,1},{2,3},{4,5},{6,7},{8,9},{10,11},{12,13},{14,15},{16,17},{18,... | collective-permute-start | bytes 245768 | tf_op jit(solution)/shard_map/ppermute | solution.py:18
  93.6 7.2 %collective-permute-start.7 = (f32[1,5,2,16,128]{4,3,2,1,0:T(8,128)}, f32[1,5,2,16,128]{4,3,2,1,0:T(8,128)}, u32[]{:S(2)}, u32[]{:S(2)}) collective-permute-start(f32[1,5,2,16,128]{4,3,2,1,0:T(8,128)} %get-tuple-element.52), channel_id=1, source_target_pairs={{1,0},{3,2},{5,4},{7,6},{9,8},{11,10},{13,12},{15,14},{17,16},{19,... | collective-permute-start | bytes 245768 | tf_op jit(solution)/shard_map/ppermute | solution.py:19
  96.6 12.4 %all-to-all-start.4 = ((f32[1,5,4,16,128]{4,2,1,0,3:T(4,128)}), f32[1,5,4,16,128]{4,2,1,0,3:T(4,128)}, u32[]{:S(2)}, u32[]{:S(2)}) async-start(f32[1,5,4,16,128]{4,2,1,0,3:T(4,128)} %copy.76), calls=%async_computation.4 | async-start | bytes 327680 | tf_op jit(solution)/shard_map/all_to_all | solution.py:89
  111.0 13.1 %all-to-all-start.5 = ((f32[16,5,4,1,128]{4,2,1,3,0:T(4,128)}), f32[16,5,4,1,128]{4,2,1,3,0:T(4,128)}, u32[]{:S(2)}, u32[]{:S(2)}) async-start(f32[16,5,4,1,128]{4,2,1,3,0:T(4,128)} %copy.78), calls=%async_computation.5 | async-start | bytes 327680 | tf_op jit(solution)/shard_map/all_to_all | solution.py:94
  129.6 8.9 %collective-permute-start.8 = (f32[1,5,2,16,128]{4,3,2,1,0:T(8,128)}, f32[1,5,2,16,128]{4,3,2,1,0:T(8,128)S(1)}, u32[]{:S(2)}, u32[]{:S(2)}) collective-permute-start(f32[1,5,2,16,128]{4,3,2,1,0:T(8,128)} %get-tuple-element.42), channel_id=1, source_target_pairs={{0,1},{2,3},{4,5},{6,7},{8,9},{10,11},{12,13},{14,15},{16,17},{18,... | collective-permute-start | bytes 245768 | tf_op jit(solution)/shard_map/ppermute | solution.py:18
  131.4 7.2 %collective-permute-start.9 = (f32[1,5,2,16,128]{4,3,2,1,0:T(8,128)}, f32[1,5,2,16,128]{4,3,2,1,0:T(8,128)}, u32[]{:S(2)}, u32[]{:S(2)}) collective-permute-start(f32[1,5,2,16,128]{4,3,2,1,0:T(8,128)} %get-tuple-element.43), channel_id=1, source_target_pairs={{1,0},{3,2},{5,4},{7,6},{9,8},{11,10},{13,12},{15,14},{17,16},{19,... | collective-permute-start | bytes 245768 | tf_op jit(solution)/shard_map/ppermute | solution.py:19
  134.4 12.4 %all-to-all-start.6 = ((f32[1,5,4,16,128]{4,2,1,0,3:T(4,128)}), f32[1,5,4,16,128]{4,2,1,0,3:T(4,128)}, u32[]{:S(2)}, u32[]{:S(2)}) async-start(f32[1,5,4,16,128]{4,2,1,0,3:T(4,128)} %copy.80), calls=%async_computation.6 | async-start | bytes 327680 | tf_op jit(solution)/shard_map/all_to_all | solution.py:89
  148.8 13.1 %all-to-all-start.7 = ((f32[16,5,4,1,128]{4,2,1,3,0:T(4,128)}), f32[16,5,4,1,128]{4,2,1,3,0:T(4,128)}, u32[]{:S(2)}, u32[]{:S(2)}) async-start(f32[16,5,4,1,128]{4,2,1,3,0:T(4,128)} %copy.82), calls=%async_computation.7 | async-start | bytes 327680 | tf_op jit(solution)/shard_map/all_to_all | solution.py:94
  167.5 8.9 %collective-permute-start.10 = (f32[1,5,2,16,128]{4,3,2,1,0:T(8,128)}, f32[1,5,2,16,128]{4,3,2,1,0:T(8,128)S(1)}, u32[]{:S(2)}, u32[]{:S(2)}) collective-permute-start(f32[1,5,2,16,128]{4,3,2,1,0:T(8,128)} %get-tuple-element.33), channel_id=1, source_target_pairs={{0,1},{2,3},{4,5},{6,7},{8,9},{10,11},{12,13},{14,15},{16,17},{18,... | collective-permute-start | bytes 245768 | tf_op jit(solution)/shard_map/ppermute | solution.py:18
  169.3 7.1 %collective-permute-start.11 = (f32[1,5,2,16,128]{4,3,2,1,0:T(8,128)}, f32[1,5,2,16,128]{4,3,2,1,0:T(8,128)}, u32[]{:S(2)}, u32[]{:S(2)}) collective-permute-start(f32[1,5,2,16,128]{4,3,2,1,0:T(8,128)} %get-tuple-element.34), channel_id=1, source_target_pairs={{1,0},{3,2},{5,4},{7,6},{9,8},{11,10},{13,12},{15,14},{17,16},{19,... | collective-permute-start | bytes 245768 | tf_op jit(solution)/shard_map/ppermute | solution.py:19
  172.2 12.4 %all-to-all-start.8 = ((f32[1,5,4,16,128]{4,2,1,0,3:T(4,128)}), f32[1,5,4,16,128]{4,2,1,0,3:T(4,128)}, u32[]{:S(2)}, u32[]{:S(2)}) async-start(f32[1,5,4,16,128]{4,2,1,0,3:T(4,128)} %copy.84), calls=%async_computation.8 | async-start | bytes 327680 | tf_op jit(solution)/shard_map/all_to_all | solution.py:89
  186.6 12.6 %all-to-all-start.9 = ((f32[16,5,4,1,128]{4,2,1,3,0:T(4,128)}), f32[16,5,4,1,128]{4,2,1,3,0:T(4,128)S(1)}, u32[]{:S(2)}, u32[]{:S(2)}) async-start(f32[16,5,4,1,128]{4,2,1,3,0:T(4,128)} %copy.86), calls=%async_computation.9 | async-start | bytes 327680 | tf_op jit(solution)/shard_map/all_to_all | solution.py:94
  (7 other events, 62.9 us)
where the time goes:
time: 205 us; the launch traced here: 202 us
  starting transfers between devices  66.9 us (33%)
  other arithmetic  63.8 us (31%)
  waiting for transfers between devices  48.2 us (24%)
  local copies, waits for them, and re-layouts  15 us (7%)
  matrix products  6.31 us (3%)
    all_to_all x5, waiting for transfers between devices, on_device(): lax.all_to_all(mixed, 'inst', split_axis=0, concat_axis=3, tiled=True)  29.7 us
    all_to_all x5, starting transfers between devices, on_device(): lax.all_to_all(section_state, 'inst', split_axis=3, concat_axis=0, tiled=...  24.4 us
    all_to_all x5, starting transfers between devices, on_device(): lax.all_to_all(mixed, 'inst', split_axis=0, concat_axis=3, tiled=True)  22.1 us
    mul x16, other arithmetic, face_terms(): second_flux = cut(second_pad, 0, length + 3) * jumps  20.8 us
    all_to_all x5, waiting for transfers between devices, on_device(): lax.all_to_all(section_state, 'inst', split_axis=3, concat_axis=0, tiled=...  18.5 us
    ppermute x6, starting transfers between devices, padded_2(): before = lax.ppermute(last, axis, up)  12.6 us
    sub x5, other arithmetic, on_device(): section_state = adjoint - section_coef * time_step[:, None] * residual  11.8 us
    reduce_sum x5, other arithmetic, on_device(): jnp.sum(jacobian[:, spatial_direction] * central[:, :, None], axis=1)  11.2 us
  transfers between devices with their start and end apart: 22, of which 10 were waited for; matrix products, arithmetic and copies ran while one was open for 23% of the time, Pallas kernels for 0%

commit v1 on v0

v1 whole, which is shorter than its diff:
```python
import functools
import math

import jax
import jax.numpy as jnp
from jax import lax
from jax.experimental import pallas as pl
from jax.experimental.pallas import tpu as pltpu
from jax.sharding import PartitionSpec as P

FACTORS = (0.25, 1.0 / 6.0, 0.375, 0.5, 1.0)
PAD = 8
MESH = pl.DeviceIdType.MESH

A_OUT, A_MIX, V1_OUT, U1_OUT, V2_BACK, V2_MIX, V3_OUT, U3_OUT, V4_BACK, V4_MIX = range(10)
UNITS = 10


def coupling_tables(count):
    slope, curve = [0.0], [count * count / 12.0 + 1.0 / 6.0]
    for m in range(1, count):
        parity = 1.0 if m % 2 == 0 else -1.0
        angle = math.pi * m / count
        slope.append(0.5 * parity * math.cos(angle) / math.sin(angle))
        curve.append(0.5 * parity / math.sin(angle) ** 2)
    return slope, curve


def kernel(
    n, cells, adj, grad, jac, c2, c4, dt, freq, damp, out,
    vp, jv, cx, cy, cz, kk, dtv, gv, zz, sx, rx, sdt, rdt, coef,
    loc_sem, ss, rs, dss, drs, hss, hrs, chs, chr_,
):
    nv, lay, ny, nz = adj.shape
    rows = lay * ny // n
    per = ny // rows
    me = lax.axis_index("inst")
    cell = lax.axis_index("cells")
    has_lo = cell > 0
    has_hi = cell < cells - 1
    mid = slice(PAD, PAD + ny)

    local = [
        (adj, vp.at[0, :, 2 : 2 + lay, mid, :]),
        (dt, dtv),
        (c2.at[0], cx.at[0, 2 : 2 + lay]),
        (c4.at[0], cx.at[1, 2 : 2 + lay]),
        (c2.at[1], cy.at[0, :, mid, :]),
        (c4.at[1], cy.at[1, :, mid, :]),
        (c2.at[2], cz.at[0]),
        (c4.at[2], cz.at[1]),
        (grad, gv),
        (jac, jv),
    ]
    local = [pltpu.make_async_copy(s, d, loc_sem.at[i]) for i, (s, d) in enumerate(local)]
    for c in local:
        c.start()

    barrier = pltpu.get_barrier_semaphore()

    @pl.loop(1, n)
    def _(r):
        pl.semaphore_signal(
            barrier, inc=1, device_id={"inst": lax.rem(me + r, n)}, device_id_type=MESH
        )

    @pl.when(has_lo)
    def _():
        pl.semaphore_signal(barrier, inc=1, device_id={"cells": cell - 1}, device_id_type=MESH)

    @pl.when(has_hi)
    def _():
        pl.semaphore_signal(barrier, inc=1, device_id={"cells": cell + 1}, device_id_type=MESH)

    slope, curve = coupling_tables(n)
    for m in range(n):
        value = freq[0] * slope[m] + damp[0] * curve[m]
        coef[m] = value
        coef[m + n] = value
    pads = jnp.zeros((nv, lay, PAD, nz), jnp.float32)
    for s in range(len(FACTORS)):
        vp[s, :, 2 : 2 + lay, 0:PAD, :] = pads
        vp[s, :, 2 : 2 + lay, PAD + ny :, :] = pads
    cy[:, :, 0:PAD, :] = jnp.zeros((2, lay, PAD, nz), jnp.float32)
    cy[:, :, PAD + ny :, :] = jnp.zeros((2, lay, PAD, nz), jnp.float32)

    @pl.when(jnp.logical_not(has_lo))
    def _():
        cx[:, 0:2] = jnp.zeros((2, 2, ny, nz), jnp.float32)
        for s in range(len(FACTORS)):
            vp[s, :, 0:2, mid, :] = jnp.zeros((nv, 2, ny, nz), jnp.float32)

    @pl.when(jnp.logical_not(has_hi))
    def _():
        cx[:, 2 + lay :] = jnp.zeros((2, 2, ny, nz), jnp.float32)
        for s in range(len(FACTORS)):
            vp[s, :, 2 + lay :, mid, :] = jnp.zeros((nv, 2, ny, nz), jnp.float32)

    pl.semaphore_wait(barrier, n - 1 + has_lo.astype(jnp.int32) + has_hi.astype(jnp.int32))

    def chunk(unit, p, slot):
        return pltpu.make_async_remote_copy(
            src_ref=sx.at[unit, p], dst_ref=rx.at[unit, slot],
            send_sem=ss.at[unit, p], recv_sem=rs.at[unit, slot],
            device_id={"inst": p}, device_id_type=MESH,
        )

    def send(unit):
        @pl.loop(1, n)
        def _(r):
            chunk(unit, lax.rem(me + r, n), me).start()

        rx[unit, me] = sx[unit, me]

    def receive(unit):
        @pl.loop(1, n)
        def _(r):
            p = lax.rem(me + r, n)
            chunk(unit, p, p).wait_recv()

    def dt_chunk(p, slot):
        return pltpu.make_async_remote_copy(
            src_ref=sdt.at[p], dst_ref=rdt.at[slot],
            send_sem=dss.at[p], recv_sem=drs.at[slot],
            device_id={"inst": p}, device_id_type=MESH,
        )

    def halo_up(s):
        return pltpu.make_async_remote_copy(
            src_ref=vp.at[s, :, lay : lay + 2, mid, :], dst_ref=vp.at[s, :, 0:2, mid, :],
            send_sem=hss.at[s, 0], recv_sem=hrs.at[s, 0],
            device_id={"cells": cell + 1}, device_id_type=MESH,
        )

    def halo_down(s):
        return pltpu.make_async_remote_copy(
            src_ref=vp.at[s, :, 2:4, mid, :], dst_ref=vp.at[s, :, 2 + lay : 4 + lay, mid, :],
            send_sem=hss.at[s, 1], recv_sem=hrs.at[s, 1],
            device_id={"cells": cell - 1}, device_id_type=MESH,
        )

    coef_up = pltpu.make_async_remote_copy(
        src_ref=cx.at[:, lay : lay + 2], dst_ref=cx.at[:, 0:2],
        send_sem=chs.at[0], recv_sem=chr_.at[0],
        device_id={"cells": cell + 1}, device_id_type=MESH,
    )
    coef_down = pltpu.make_async_remote_copy(
        src_ref=cx.at[:, 2:4], dst_ref=cx.at[:, 2 + lay : 4 + lay],
        send_sem=chs.at[1], recv_sem=chr_.at[1],
        device_id={"cells": cell - 1}, device_id_type=MESH,
    )

    def start_pair(up, down):
        @pl.when(has_hi)
        def _():
            up.start()

        @pl.when(has_lo)
        def _():
            down.start()

    def land_pair(up, down):
        @pl.when(has_lo)
        def _():
            up.wait_recv()

        @pl.when(has_hi)
        def _():
            down.wait_recv()

    def sent_pair(up, down):
        @pl.when(has_hi)
        def _():
            up.wait_send()

        @pl.when(has_lo)
        def _():
            down.wait_send()

    def pieces(body):
        @pl.loop(0, lay)
        def _(x):
            for q in range(per):
                for b in range(nv):
                    body(
                        x, x * per + q, b, slice(b * rows, (b + 1) * rows),
                        slice(q * rows, (q + 1) * rows),
                        slice(PAD + q * rows, PAD + (q + 1) * rows),
                    )

    def pack(s, unit):
        def body(x, d, b, chunk_rows, plain, padded):
            sx[unit, d, chunk_rows, :] = vp[s, b, 2 + x, padded, :]

        pieces(body)

    def unpack(unit, s):
        def body(x, d, b, chunk_rows, plain, padded):
            vp[s, b, 2 + x, padded, :] = rx[unit, d, chunk_rows, :]

        pieces(body)

    def finish(unit, s):
        factor = FACTORS[s - 1]

        def body(x, d, b, chunk_rows, plain, padded):
            vp[s, b, 2 + x, padded, :] = zz[b, x, plain, :] - (factor * dtv[x, plain, :]) * rx[
                unit, d, chunk_rows, :
            ]

        pieces(body)

    lanes = lax.broadcasted_iota(jnp.int32, (ny, nz), 1)
    half_lo = jnp.where(lanes >= 1, 0.5, 0.0)
    half_hi = jnp.where(lanes < nz - 1, 0.5, 0.0)

    def stencil():
        @pl.loop(0, lay)
        def _(x):
            up4 = cx[1, x + 3]
            here3 = 3.0 * cx[1, x + 2] + cx[0, x + 2]
            below3 = 3.0 * cx[1, x + 1] + cx[0, x + 1]
            below4 = cx[1, x]
            kk[0, x] = below4
            kk[1, x] = -(below3 + below4)
            kk[2, x] = -(up4 + here3)
            kk[3, x] = up4
            centre = here3 + below3
            up4 = cy[1, x, PAD + 1 : PAD + 1 + ny, :]
            here3 = 3.0 * cy[1, x, mid, :] + cy[0, x, mid, :]
            low = slice(PAD - 1, PAD - 1 + ny)
            below3 = 3.0 * cy[1, x, low, :] + cy[0, x, low, :]
            below4 = cy[1, x, PAD - 2 : PAD - 2 + ny, :]
            kk[4, x] = below4
            kk[5, x] = -(below3 + below4)
            kk[6, x] = -(up4 + here3)
            kk[7, x] = up4
            centre = centre + here3 + below3
            here4 = cz[1, x]
            here3 = 3.0 * here4 + cz[0, x]
            up4 = jnp.where(lanes < nz - 1, pltpu.roll(here4, nz - 1, 1), 0.0)
            below3 = jnp.where(lanes >= 1, pltpu.roll(here3, 1, 1), 0.0)
            below4 = jnp.where(lanes >= 2, pltpu.roll(here4, 2, 1), 0.0)
            kk[8, x] = below4
            kk[9, x] = jnp.where(lanes >= 1, -(below3 + below4), 0.0)
            kk[10, x] = jnp.where(lanes < nz - 1, -(up4 + here3), 0.0)
            kk[11, x] = jnp.where(lanes < nz - 2, up4, 0.0)
            kk[12, x] = centre + here3 + below3

    def spatial(s, emit):
        factor = FACTORS[s]

        @pl.loop(0, lay)
        def _(x):
            sums, central = [], [[], [], []]
            for b in range(nv):
                v0 = vp[s, b, x + 2, mid, :]
                total = kk[12, x] * v0
                m2, m1 = vp[s, b, x, mid, :], vp[s, b, x + 1, mid, :]
                p1, p2 = vp[s, b, x + 3, mid, :], vp[s, b, x + 4, mid, :]
                total += kk[0, x] * m2 + kk[1, x] * m1 + kk[2, x] * p1 + kk[3, x] * p2
                central[0].append(0.5 * (m1 - p1))
                m2, m1, p1, p2 = (
                    vp[s, b, x + 2, PAD + o : PAD + o + ny, :] for o in (-2, -1, 1, 2)
                )
                total += kk[4, x] * m2 + kk[5, x] * m1 + kk[6, x] * p1 + kk[7, x] * p2
                central[1].append(0.5 * (m1 - p1))
                m2, m1, p1, p2 = (pltpu.roll(v0, o, 1) for o in (2, 1, nz - 1, nz - 2))
                total += kk[8, x] * m2 + kk[9, x] * m1 + kk[10, x] * p1 + kk[11, x] * p2
                central[2].append(half_lo * m1 - half_hi * p1)
                sums.append(total)
            step = factor * dtv[x]
            for b in range(nv):
                total = sums[b] + gv[b, x]
                for d in range(3):
                    for a in range(nv):
                        total += jv[d, a, b, x] * central[d][a]
                emit(x, b, vp[0, b, x + 2, mid, :] - step * total)

    def to_home(x, b, value):
        zz[b, x] = value

    def to_chunks(unit):
        def emit(x, b, value):
            for q in range(per):
                sx[unit, x * per + q, b * rows : (b + 1) * rows, :] = value[
                    q * rows : (q + 1) * rows
                ]

        return emit

    def mix(source, target):
        @pl.loop(0, n)
        def _(k):
            total = coef[n - k] * source(0)
            for j in range(1, n):
                total += coef[n + j - k] * source(j)
            target(k, total)

    local[0].wait()
    pack(0, A_OUT)
    send(A_OUT)
    start_pair(halo_up(0), halo_down(0))
    local[2].wait()
    local[3].wait()
    start_pair(coef_up, coef_down)
    local[1].wait()

    @pl.loop(0, lay)
    def _(x):
        for q in range(per):
            sdt[x * per + q] = dtv[x, q * rows : (q + 1) * rows, :]

    @pl.loop(1, n)
    def _(r):
        dt_chunk(lax.rem(me + r, n), me).start()

    rdt[me] = sdt[me]
    for c in local[4:]:
        c.wait()
    land_pair(coef_up, coef_down)
    stencil()
    land_pair(halo_up(0), halo_down(0))
    spatial(0, to_home)
    receive(A_OUT)

    def store(unit):
        def target(k, value):
            sx[unit, k] = value

        return target

    mix(lambda j: rx[A_OUT, j], store(A_MIX))
    send(A_MIX)

    @pl.loop(1, n)
    def _(r):
        p = lax.rem(me + r, n)
        dt_chunk(p, p).wait_recv()

    receive(A_MIX)
    finish(A_MIX, 1)

    for s, v_out, u_out, v_back, v_mix in (
        (1, V1_OUT, U1_OUT, V2_BACK, V2_MIX),
        (3, V3_OUT, U3_OUT, V4_BACK, V4_MIX),
    ):
        pack(s, v_out)
        start_pair(halo_up(s), halo_down(s))
        send(v_out)
        land_pair(halo_up(s), halo_down(s))
        spatial(s, to_chunks(u_out))
        send(u_out)
        receive(v_out)
        receive(u_out)

        def advance(k, value, s=s, u_out=u_out, v_back=v_back):
            step = FACTORS[s] * rdt[k]
            for b in range(nv):
                part = slice(b * rows, (b + 1) * rows)
                sx[v_back, k, part, :] = rx[u_out, k, part, :] - step * value[part]

        mix(lambda j: rx[v_out, j], advance)
        send(v_back)
        mix(lambda j: sx[v_back, j], store(v_mix))
        send(v_mix)
        receive(v_back)
        unpack(v_back, s + 1)
        start_pair(halo_up(s + 1), halo_down(s + 1))
        land_pair(halo_up(s + 1), halo_down(s + 1))
        spatial(s + 1, to_home)
        receive(v_mix)
        if s + 2 < len(FACTORS):
            finish(v_mix, s + 2)

    def last(x, d, b, chunk_rows, plain, padded):
        out[b, x, plain, :] = zz[b, x, plain, :] - (FACTORS[-1] * dtv[x, plain, :]) * rx[
            V4_MIX, d, chunk_rows, :
        ]

    pieces(last)

    @pl.loop(1, n)
    def _(r):
        p = lax.rem(me + r, n)
        dt_chunk(p, me).wait_send()
        for unit in range(UNITS):
            chunk(unit, p, me).wait_send()

    for s in range(len(FACTORS)):
        sent_pair(halo_up(s), halo_down(s))
    sent_pair(coef_up, coef_down)


def on_device(n, cells, adjoint, grad, jac, c2, c4, dt, freq, damp):
    nv, lay, ny, nz = adjoint.shape[1:]
    rows = lay * ny // n
    assert rows * n == lay * ny and ny % rows == 0 and lay >= 2
    f32 = jnp.float32
    anywhere = pl.BlockSpec(memory_space=pl.ANY)
    scalar = pl.BlockSpec(memory_space=pltpu.SMEM)
    sections = len(FACTORS)
    dma = pltpu.SemaphoreType.DMA
    tall = ny + 2 * PAD
    result = pl.pallas_call(
        functools.partial(kernel, n, cells),
        out_shape=jax.ShapeDtypeStruct(adjoint.shape[1:], f32),
        in_specs=[anywhere] * 6 + [scalar] * 2,
        out_specs=pl.BlockSpec(memory_space=pltpu.VMEM),
        scratch_shapes=[
            pltpu.VMEM((sections, nv, lay + 4, tall, nz), f32),
            pltpu.VMEM(jac.shape[1:], f32),
            pltpu.VMEM((2, lay + 4, ny, nz), f32),
            pltpu.VMEM((2, lay, tall, nz), f32),
            pltpu.VMEM((2, lay, ny, nz), f32),
            pltpu.VMEM((13, lay, ny, nz), f32),
            pltpu.VMEM((lay, ny, nz), f32),
            pltpu.VMEM((nv, lay, ny, nz), f32),
            pltpu.VMEM((nv, lay, ny, nz), f32),
            pltpu.VMEM((UNITS, n, nv * rows, nz), f32),
            pltpu.VMEM((UNITS, n, nv * rows, nz), f32),
            pltpu.VMEM((n, rows, nz), f32),
            pltpu.VMEM((n, rows, nz), f32),
            pltpu.SMEM((2 * n,), f32),
            dma((10,)),
            dma((UNITS, n)),
            dma((UNITS, n)),
            dma((n,)),
            dma((n,)),
            dma((sections, 2)),
            dma((sections, 2)),
            dma((2,)),
            dma((2,)),
        ],
        compiler_params=pltpu.CompilerParams(collective_id=0, has_side_effects=True),
    )(adjoint[0], grad[0], jac[0], c2[0], c4[0], dt[0], freq, damp)
    return result[None]


def solution(mesh):
    placed = (
        P("inst", None, "cells", None, None),
        P("inst", None, "cells", None, None),
        P("inst", None, None, None, "cells", None, None),
        P("inst", None, "cells", None, None),
        P("inst", None, "cells", None, None),
        P("inst", "cells", None, None),
        P(),
        P(),
    )
    return jax.shard_map(
        functools.partial(on_device, mesh.shape["inst"], mesh.shape["cells"]),
        mesh=mesh,
        in_specs=placed,
        out_specs=P("inst", None, "cells", None, None),
        check_vma=False,
    )
```

time: 205 us -> 63.5 us (0.31); the launches traced: 202 us -> 63.3 us
  starting transfers between devices: 66.9 us -> 0 us
  other arithmetic: 63.8 us -> 0 us
  Pallas kernels: 0 us -> 60.4 us
  waiting for transfers between devices: 48.2 us -> 0 us
  local copies, waits for them, and re-layouts: 15 us -> 1.59 us
  matrix products: 6.31 us -> 0 us
    pallas_call x0 -> x1, Pallas kernels: none -> 60.4 us  [on_device(): pl.pallas_call(functools.partial(kernel, n, cells), out_shape=jax.ShapeDt...]
    all_to_all x10 -> x0, waiting for transfers between devices: 48.2 us -> none  [the longest x5 29.7 us: on_device(): lax.all_to_all(mixed, 'inst', split_axis=0, concat_axis=3, tiled=True)]
    all_to_all x10 -> x0, starting transfers between devices: 46.5 us -> none  [the longest x5 24.4 us: on_device(): lax.all_to_all(section_state, 'inst', split_axis=3, concat_axis=0, tiled=...]
    mul x22 -> x0, other arithmetic: 29.1 us -> none  [the longest x16 20.8 us: face_terms(): second_flux = cut(second_pad, 0, length + 3) * jumps]
    ppermute x12 -> x0, starting transfers between devices: 20.4 us -> none  [the longest x6 12.6 us: padded_2(): before = lax.ppermute(last, axis, up)]
    sub x20 -> x0, other arithmetic: 19.3 us -> none  [the longest x5 11.8 us: on_device(): section_state = adjoint - section_coef * time_step[:, None] * residual]
    reduce_sum x5 -> x0, other arithmetic: 11.2 us -> none  [on_device(): jnp.sum(jacobian[:, spatial_direction] * central[:, :, None], axis=1)]
    dot_general x5 -> x0, matrix products: 6.31 us -> none  [on_device(): jnp.einsum('jk,jvxyz->kvxyz', coupling, lax.all_to_all(section_state, 'in...]
  transfers between devices with their start and end apart: 22 -> 0, of which waited for: 10 -> 0; matrix products, arithmetic and copies ran while one was open for 23% -> 0% of each run, Pallas kernels for 0% -> 0%
where the time goes in v1:
time: 63.5 us; the launch traced here: 63.3 us
  Pallas kernels  60.4 us (95%)
  local copies, waits for them, and re-layouts  1.59 us (3%)
  between operations  1.3 us (2%)
    pallas_call x1, Pallas kernels, on_device(): pl.pallas_call(functools.partial(kernel, n, cells), out_shape=jax.ShapeDt...  60.4 us
    unnamed x1, local copies, waits for them, and re-layouts  1.59 us

profile of v1, /device:TPU:0, one launch (start us, length us, event | category | flops | bytes accessed | tf_op | source)
XLA Modules:
  0.0 63.3 jit_solution(14964697997812188856)
XLA Ops:
  1.3 60.4 %shard_map.82 = f32[5,4,16,128]{3,2,1,0:T(8,128)} custom-call(f32[5,4,16,128]{3,2,1,0:T(8,128)} %bitcast.9, f32[5,4,16,128]{3,2,1,0:T(8,128)} %bitcast.10, f32[3,5,5,4,16,128]{5,4,3,2,1,0:T(8,128)} %bitcast.7, f32[3,4,16,128]{3,2,1,0:T(8,128)} %bitcast.11, f32[3,4,16,128]{3,2,1,0:T(8,128)} %bitcast.12, f32[4,16,128]{2,1,0:T(8,128)} %bitcast.13, ...), custom_call_target="tpu_custom_call" | custom-call | tf_op jit(solution)/shard_map/pallas_call | solution.py:405
  61.7 1.6 %copy.12 = f32[1,5,4,16,128]{4,3,2,1,0:T(8,128)} copy(f32[1,5,4,16,128]{4,3,2,1,0:T(8,128)} %bitcast.8) | data formatting | bytes 327680

commit v2 on v1

--- a/solution.py
+++ b/solution.py
@@ -27,8 +27,8 @@
 
 
 def kernel(
-    n, cells, adj, grad, jac, c2, c4, dt, freq, damp, out,
-    vp, jv, cx, cy, cz, kk, dtv, gv, zz, sx, rx, sdt, rdt, coef,
+    n, cells, adj, grad, jac, c2, c4, dt, freq_in, damp_in, out,
+    vp, jv, cx, cy, cz, kk, dtv, gv, zz, sx, rx, mm, sdt, rdt, coef, freq, damp,
     loc_sem, ss, rs, dss, drs, hss, hrs, chs, chr_,
 ):
     nv, lay, ny, nz = adj.shape
@@ -51,6 +51,8 @@
         (c4.at[2], cz.at[1]),
         (grad, gv),
         (jac, jv),
+        (freq_in, freq),
+        (damp_in, damp),
     ]
     local = [pltpu.make_async_copy(s, d, loc_sem.at[i]) for i, (s, d) in enumerate(local)]
     for c in local:
@@ -73,6 +75,8 @@
         pl.semaphore_signal(barrier, inc=1, device_id={"cells": cell + 1}, device_id_type=MESH)
 
     slope, curve = coupling_tables(n)
+    local[10].wait()
+    local[11].wait()
     for m in range(n):
         value = freq[0] * slope[m] + damp[0] * curve[m]
         coef[m] = value
@@ -96,7 +100,13 @@
         for s in range(len(FACTORS)):
             vp[s, :, 2 + lay :, mid, :] = jnp.zeros((nv, 2, ny, nz), jnp.float32)
 
-    pl.semaphore_wait(barrier, n - 1 + has_lo.astype(jnp.int32) + has_hi.astype(jnp.int32))
+    half = n // 2
+
+    def partner(i):
+        own = i // half
+        return lax.rem(me // half + 1 + own, 2) * half + lax.rem(
+            lax.rem(me, half) + i + own, half
+        )
 
     def chunk(unit, p, slot):
         return pltpu.make_async_remote_copy(
@@ -106,9 +116,9 @@
         )
 
     def send(unit):
-        @pl.loop(1, n)
-        def _(r):
-            chunk(unit, lax.rem(me + r, n), me).start()
+        @pl.loop(0, n - 1)
+        def _(i):
+            chunk(unit, partner(i), me).start()
 
         rx[unit, me] = sx[unit, me]
 
@@ -249,9 +259,17 @@
 
     def spatial(s, emit):
         factor = FACTORS[s]
+        both = has_lo.astype(jnp.int32) * has_hi.astype(jnp.int32)
+        back = has_lo.astype(jnp.int32) * (1 - both)
+        late = (lay - 2) * (1 - both)
 
         @pl.loop(0, lay)
-        def _(x):
+        def _(i):
+            @pl.when(i == late)
+            def _():
+                land_pair(halo_up(s), halo_down(s))
+
+            x = back * (lay - 1 - i) + (1 - back) * i
             sums, central = [], [[], [], []]
             for b in range(nv):
                 v0 = vp[s, b, x + 2, mid, :]
@@ -289,16 +307,30 @@
 
         return emit
 
-    def mix(source, target):
-        @pl.loop(0, n)
-        def _(k):
-            total = coef[n - k] * source(0)
-            for j in range(1, n):
-                total += coef[n + j - k] * source(j)
-            target(k, total)
+    def mixed(source, k):
+        total = coef[n - k] * source(0)
+        for j in range(1, n):
+            total += coef[n + j - k] * source(j)
+        return total
+
+    def form_and_send(unit, form):
+        @pl.loop(0, n - 1)
+        def _(i):
+            p = partner(i)
+            sx[unit, p] = form(p)
+
+            @pl.when(i > 0)
+            def _():
+                chunk(unit, partner(i - 1), me).start()
+
+        value = form(me)
+        sx[unit, me] = value
+        rx[unit, me] = value
+        chunk(unit, partner(n - 2), me).start()
 
     local[0].wait()
     pack(0, A_OUT)
+    pl.semaphore_wait(barrier, n - 1 + has_lo.astype(jnp.int32) + has_hi.astype(jnp.int32))
     send(A_OUT)
     start_pair(halo_up(0), halo_down(0))
     local[2].wait()
@@ -316,22 +348,14 @@
         dt_chunk(lax.rem(me + r, n), me).start()
 
     rdt[me] = sdt[me]
-    for c in local[4:]:
+    for c in local[4:10]:
         c.wait()
     land_pair(coef_up, coef_down)
     stencil()
-    land_pair(halo_up(0), halo_down(0))
     spatial(0, to_home)
     receive(A_OUT)
 
-    def store(unit):
-        def target(k, value):
-            sx[unit, k] = value
-
-        return target
-
-    mix(lambda j: rx[A_OUT, j], store(A_MIX))
-    send(A_MIX)
+    form_and_send(A_MIX, lambda k: mixed(lambda j: rx[A_OUT, j], k))
 
     @pl.loop(1, n)
     def _(r):
@@ -345,29 +369,30 @@
         (1, V1_OUT, U1_OUT, V2_BACK, V2_MIX),
         (3, V3_OUT, U3_OUT, V4_BACK, V4_MIX),
     ):
+        start_pair(halo_up(s), halo_down(s))
         pack(s, v_out)
-        start_pair(halo_up(s), halo_down(s))
         send(v_out)
-        land_pair(halo_up(s), halo_down(s))
         spatial(s, to_chunks(u_out))
         send(u_out)
         receive(v_out)
-        receive(u_out)
-
-        def advance(k, value, s=s, u_out=u_out, v_back=v_back):
+
+        @pl.loop(0, n)
+        def _(k):
+            mm[k] = mixed(lambda j: rx[v_out, j], k)
+
+        def advance(k, s=s, u_out=u_out):
+            @pl.when(k != me)
+            def _():
+                chunk(u_out, k, k).wait_recv()
+
             step = FACTORS[s] * rdt[k]
-            for b in range(nv):
-                part = slice(b * rows, (b + 1) * rows)
-                sx[v_back, k, part, :] = rx[u_out, k, part, :] - step * value[part]
-
-        mix(lambda j: rx[v_out, j], advance)
-        send(v_back)
-        mix(lambda j: sx[v_back, j], store(v_mix))
-        send(v_mix)
+            return rx[u_out, k] - jnp.concatenate([step] * nv, axis=0) * mm[k]
+
+        form_and_send(v_back, advance)
+        form_and_send(v_mix, lambda k: mixed(lambda j: sx[v_back, j], k))
         receive(v_back)
         unpack(v_back, s + 1)
         start_pair(halo_up(s + 1), halo_down(s + 1))
-        land_pair(halo_up(s + 1), halo_down(s + 1))
         spatial(s + 1, to_home)
         receive(v_mix)
         if s + 2 < len(FACTORS):
@@ -398,14 +423,13 @@
     assert rows * n == lay * ny and ny % rows == 0 and lay >= 2
     f32 = jnp.float32
     anywhere = pl.BlockSpec(memory_space=pl.ANY)
-    scalar = pl.BlockSpec(memory_space=pltpu.SMEM)
     sections = len(FACTORS)
     dma = pltpu.SemaphoreType.DMA
     tall = ny + 2 * PAD
     result = pl.pallas_call(
         functools.partial(kernel, n, cells),
         out_shape=jax.ShapeDtypeStruct(adjoint.shape[1:], f32),
-        in_specs=[anywhere] * 6 + [scalar] * 2,
+        in_specs=[anywhere] * 8,
         out_specs=pl.BlockSpec(memory_space=pltpu.VMEM),
         scratch_shapes=[
             pltpu.VMEM((sections, nv, lay + 4, tall, nz), f32),
@@ -419,10 +443,13 @@
             pltpu.VMEM((nv, lay, ny, nz), f32),
             pltpu.VMEM((UNITS, n, nv * rows, nz), f32),
             pltpu.VMEM((UNITS, n, nv * rows, nz), f32),
+            pltpu.VMEM((n, nv * rows, nz), f32),
             pltpu.VMEM((n, rows, nz), f32),
             pltpu.VMEM((n, rows, nz), f32),
             pltpu.SMEM((2 * n,), f32),
-            dma((10,)),
+            pltpu.SMEM((1,), f32),
+            pltpu.SMEM((1,), f32),
+            dma((12,)),
             dma((UNITS, n)),
             dma((UNITS, n)),
             dma((n,)),

time: 63.5 us -> 61.8 us (0.973)
  Pallas kernels: 60.4 us -> 58.7 us
    pallas_call x1, Pallas kernels: 60.4 us -> 58.7 us  [on_device(): pl.pallas_call(functools.partial(kernel, n, cells), out_shape=jax.ShapeDt...]
where the time goes in v2:
time: 61.8 us; the launch traced here: 61.6 us
  Pallas kernels  58.7 us (95%)
  local copies, waits for them, and re-layouts  1.59 us (3%)
  between operations  1.3 us (2%)
    pallas_call x1, Pallas kernels, on_device(): pl.pallas_call(functools.partial(kernel, n, cells), out_shape=jax.ShapeDt...  58.7 us
    unnamed x1, local copies, waits for them, and re-layouts  1.59 us

profile of v2, /device:TPU:0, one launch (start us, length us, event | category | flops | bytes accessed | tf_op | source)
XLA Modules:
  0.0 61.6 jit_solution(12802876579286380860)
XLA Ops:
  1.3 58.7 %shard_map.82 = f32[5,4,16,128]{3,2,1,0:T(8,128)} custom-call(f32[5,4,16,128]{3,2,1,0:T(8,128)} %bitcast.9, f32[5,4,16,128]{3,2,1,0:T(8,128)} %bitcast.10, f32[3,5,5,4,16,128]{5,4,3,2,1,0:T(8,128)} %bitcast.7, f32[3,4,16,128]{3,2,1,0:T(8,128)} %bitcast.11, f32[3,4,16,128]{3,2,1,0:T(8,128)} %bitcast.12, f32[4,16,128]{2,1,0:T(8,128)} %bitcast.13, ...), custom_call_target="tpu_custom_call" | custom-call | tf_op jit(solution)/shard_map/pallas_call | solution.py:429
  60.0 1.6 %copy.12 = f32[1,5,4,16,128]{4,3,2,1,0:T(8,128)} copy(f32[1,5,4,16,128]{4,3,2,1,0:T(8,128)} %bitcast.8) | data formatting | bytes 327680
